TPU v7x, 512 devices: a whole 4x4x16 slice. The times are simulated.
512 devices in a mesh: expert: 16 (over z), shard: 32 (over y, x, core).
Axes of the slice: x: 4, y: 4, z: 16, core: 2. Of those that a mesh axis runs over, the one named last changes fastest.
Arguments:
- tokens: bfloat16 [384, 6144], P('expert', 'shard'), may hold values from -6 to 6
- routes: int32 [384, 2], P('expert'), may hold values from 0 to 7, all different within a row; in each aligned block of 24 rows (0 to 23, 24 to 47, ...) at most 12 rows name the same one
- w_router: bfloat16 [6144, 8], replicated, may hold values from -0.078125 to 0.078125
- w_gate: bfloat16 [6144, 65536], P(None, ('expert', 'shard')), may hold values from -0.078125 to 0.078125
- w_up: bfloat16 [6144, 65536], P(None, ('expert', 'shard')), may hold values from -0.078125 to 0.078125
- w_down: bfloat16 [65536, 6144], P(('expert', 'shard')), may hold values from -0.25 to 0.25
Outputs:
- mixed: bfloat16 [384, 6144], P('expert', 'shard')
Inputs may be any that keep to these rules, and one draw needn't show every extreme that they name: `routes`: the two experts of a row differ; within each aligned block of 24 rows no expert is named more than 24 / 2 times, and some expert is named exactly that often.
All inputs are finite; a program needn't handle non-finite values.
Results may differ from a plain program's by a relative error of at most 0.017.
Values may be sent and summed in bfloat16 or wider, within the bound.
No kernel may reach another device: no remote copies, remote signals or barrier semaphores. Data moves between devices by JAX's collectives and lax.ppermute only.
A program may use at most 128 MiB of HBM per device.

v0:
```python
import jax
import jax.numpy as jnp
from jax import lax
from jax.sharding import PartitionSpec as P

FF_W = 8192


def sent_to_all(value, axis):
    peers = lax.axis_size(axis)
    return lax.all_to_all(
        jnp.broadcast_to(value[None], (peers, *value.shape)), axis, 0, 0, tiled=True
    )


def of_everyone(value, axis):
    everything = sent_to_all(value, axis)
    return jnp.sum(everything, axis=0)


def joined_along(blocks, dim):
    blocks = jnp.moveaxis(blocks, 0, dim)
    dims = blocks.shape
    return blocks.reshape(*dims[:dim], dims[dim] * dims[dim + 1], *dims[dim + 2 :])


def gather_directly(value, axis, dim):
    return joined_along(sent_to_all(value, axis), dim)


def cut_along(value, dim, peers):
    before, after = (value.shape[:dim], value.shape[dim + 1 :])
    return jnp.moveaxis(value.reshape(*before, peers, -1, *after), dim, 0)


def sum_at_owner(value, axis, dim):
    blocks = cut_along(value, dim, lax.axis_size(axis))
    arrived = lax.all_to_all(blocks, axis, split_axis=0, concat_axis=0, tiled=True)
    return arrived.astype(jnp.float32).sum(axis=0)


def local(tokens, routes, w_router, w_gate, w_up, w_down):
    tok_dev, dpiece = tokens.shape
    experts = w_router.shape[1]
    capacity = tok_dev // 2
    groups = lax.axis_size("expert")
    shards = lax.axis_size("shard")
    repeat = max(1, groups // experts)
    per_group = max(1, experts // groups)
    width = w_gate.shape[1]
    group_idx = lax.axis_index("expert")
    shard_idx = lax.axis_index("shard")
    expert_here = (group_idx * shards + shard_idx) * width // FF_W
    local_k = expert_here % per_group
    flat = routes.reshape(-1)
    onehot = (flat[:, None] == jnp.arange(experts)[None, :]).astype(jnp.int32)
    rank = jnp.cumsum(onehot, axis=0) - onehot
    slot = jnp.sum(rank * onehot, axis=1)
    target = flat * capacity + slot
    place = (target[:, None] == jnp.arange(experts * capacity)[None, :]).reshape(
        tok_dev, 2, experts * capacity
    )
    dispatch = jnp.any(place, axis=1).T.astype(jnp.bfloat16)
    rows_total = groups * capacity
    router_piece = lax.dynamic_slice_in_dim(w_router, shard_idx * dpiece, dpiece, 0)
    logits = of_everyone(jnp.dot(tokens, router_piece, preferred_element_type=jnp.float32), "shard")
    bucket = jnp.dot(dispatch, tokens, preferred_element_type=jnp.float32).astype(jnp.bfloat16)
    spread = jnp.repeat(bucket.reshape(experts, capacity, -1), repeat, axis=0)
    arrived = lax.all_to_all(
        spread.reshape(groups, per_group, capacity, -1),
        "expert",
        split_axis=0,
        concat_axis=0,
        tiled=True,
    )
    piece = gather_directly(arrived, "shard", 3)
    count = piece.shape[3]
    chosen = lax.dynamic_index_in_dim(piece, local_k, 1, keepdims=False).reshape(rows_total, count)
    gate = jnp.dot(chosen, w_gate, preferred_element_type=jnp.float32)
    up = jnp.dot(chosen, w_up, preferred_element_type=jnp.float32)
    hidden = (jax.nn.silu(gate) * up).astype(jnp.bfloat16)
    partial_out = jnp.dot(hidden, w_down, preferred_element_type=jnp.float32)
    keep = jnp.arange(per_group) == local_k
    term = jnp.where(keep[None, :, None, None], partial_out.reshape(groups, 1, capacity, -1), 0.0)
    shares = sum_at_owner(term.astype(jnp.bfloat16), "shard", 3)
    back = lax.all_to_all(
        shares.astype(jnp.bfloat16), "expert", split_axis=0, concat_axis=0, tiled=True
    )
    expert_out = jnp.sum(
        back.astype(jnp.float32).reshape(experts, repeat, capacity, dpiece), axis=1
    )
    expert_out = expert_out.reshape(experts * capacity, dpiece)
    picks = jnp.sum(
        jnp.where(
            routes[:, :, None] == jnp.arange(experts)[None, None, :], logits[:, None, :], 0.0
        ),
        axis=2,
    )
    first = 1.0 / (1.0 + jnp.exp(picks[:, 1] - picks[:, 0]))
    second = 1.0 / (1.0 + jnp.exp(picks[:, 0] - picks[:, 1]))
    weights = jnp.stack([first, second], axis=1)
    combine = jnp.sum(jnp.where(place, weights[:, :, None], 0.0), axis=1)
    mixed = jnp.dot(
        combine, expert_out, precision=lax.Precision.HIGHEST, preferred_element_type=jnp.float32
    )
    return mixed.astype(jnp.bfloat16)


def solution(mesh):
    return jax.shard_map(
        local,
        mesh=mesh,
        in_specs=(
            P("expert", "shard"),
            P("expert", None),
            P(),
            P(None, ("expert", "shard")),
            P(None, ("expert", "shard")),
            P(("expert", "shard"), None),
        ),
        out_specs=P("expert", "shard"),
        check_vma=False,
    )
```

profile of v0, /device:TPU:32, one launch (start us, length us, event | category | flops | bytes accessed | tf_op | source)
XLA Modules:
  0.0 189.0 jit_solution(6360991764029700150)
XLA Ops:
  0.0 0.0 copy-start
  0.0 0.9 copy.51
  0.9 0.1 eq.23
  1.0 0.1 fusion.8
  1.1 0.1 reduce_window_sum.11
  1.1 0.2 select_reduce_fusion.1
  1.3 0.1 reduce_sum.62
  1.4 0.1 copy.52
  1.5 0.7 multiply_add_fusion
  2.2 0.1 fusion.7
  2.3 0.9 convolution_convert_fusion.1
  3.2 29.2 %all_to_all.25 = bf16[16,1,12,192]{3,2,1,0:T(8,128)(2,1)S(1)} all-to-all(bf16[16,1,12,192]{3,2,1,0:T(8,128)(2,1)S(1)} %bitcast.34), channel_id=1, replica_groups=mesh['expert'=16,'shard'=32] {'expert'}, dimensions={0} | all-to-all | bytes 147456 | tf_op jit(solution)/shard_map/all_to_all | solution.py:69
  32.5 2.1 %broadcast_in_dim.64 = bf16[32,16,1,12,192]{4,1,3,2,0:T(8,128)(2,1)} broadcast(bf16[16,12,192]{2,0,1:T(8,128)(2,1)S(1)} %copy.53), dimensions={1,3,4} | broadcast | bytes 2433024 | tf_op jit(solution)/shard_map/broadcast_in_dim | solution.py:12
  34.5 0.0 copy-start.2
  34.5 7.6 %all-to-all-start.2 = ((bf16[32,16,1,12,192]{4,1,3,2,0:T(8,128)(2,1)}), bf16[32,16,1,12,192]{4,1,3,2,0:T(8,128)(2,1)}, u32[]{:S(2)}, u32[]{:S(2)}) async-start(bf16[32,16,1,12,192]{4,1,3,2,0:T(8,128)(2,1)} %broadcast_in_dim.64), calls=%async_computation.2 | async-start | bytes 6291456 | tf_op jit(solution)/shard_map/all_to_all | solution.py:11
  42.1 0.0 copy-done.2
  42.1 0.9 convolution_bitcast_fusion
  43.0 0.7 reshape.73
  43.8 40.1 %all-to-all-done.2 = bf16[32,16,1,12,192]{4,1,3,2,0:T(8,128)(2,1)} async-done(((bf16[32,16,1,12,192]{4,1,3,2,0:T(8,128)(2,1)}), bf16[32,16,1,12,192]{4,1,3,2,0:T(8,128)(2,1)}, u32[]{:S(2)}, u32[]{:S(2)}) %all-to-all-start.2) | async-done | bytes 2359328 | tf_op jit(solution)/shard_map/all_to_all | solution.py:11
  83.9 3.8 %all-to-all-start = ((f32[32,1,192]{2,1,0:T(1,128)}), f32[32,1,192]{2,1,0:T(1,128)S(1)}, u32[]{:S(2)}, u32[]{:S(2)}) async-start(f32[32,1,192]{2,1,0:T(1,128)} %reshape.73), calls=%async_computation | async-start | bytes 65536 | tf_op jit(solution)/shard_map/all_to_all | solution.py:11
  87.7 5.4 %copy.54 = bf16[16,1,12,32,192]{4,3,2,0,1:T(8,128)(2,1)} copy(bf16[16,1,12,32,192]{4,0,2,1,3:T(8,128)(2,1)} %bitcast.3) | data formatting | bytes 4718592 | tf_op jit(solution)/shard_map/transpose | solution.py:22
  93.0 0.0 copy-start.1
  93.0 6.3 %reshape.67 = bf16[192,6144]{1,0:T(8,128)(2,1)} reshape(bf16[16,1,12,32,192]{4,3,2,0,1:T(8,128)(2,1)} %copy.54) | data formatting | bytes 4718592 | tf_op jit(solution)/shard_map/reshape | solution.py:78
  99.4 0.0 copy-done.1
  99.4 2.4 %fusion.12 = f32[192,128]{1,0:T(8,128)S(1)} fusion(bf16[192,6144]{1,0:T(8,128)(2,1)} %reshape.67, bf16[6144,128]{1,0:T(8,128)(2,1)S(1)} %copy-done.1), kind=kOutput, calls=%fused_computation.31 | convolution fusion | flops 301989888 | bytes 4030464 | tf_op jit(solution)/shard_map/dot_general | solution.py:79
  101.8 0.0 copy-done
  101.8 5.0 %convolution_convert_fusion = bf16[192,6144]{1,0:T(8,128)(2,1)} fusion(bf16[128,6144]{1,0:T(8,128)(2,1)S(1)} %copy-done, bf16[192,6144]{1,0:T(8,128)(2,1)} %reshape.67, bf16[6144,128]{1,0:T(8,128)(2,1)} %param.10, f32[192,128]{1,0:T(8,128)S(1)} %fusion.12), kind=kOutput, calls=%fused_computation | convolution fusion | flops 605306880 | bytes 7962624 | tf_op jit(solution)/shard_map/dot_general | solution.py:82
  106.8 6.4 %convert_element_type.35 = bf16[16,1,12,32,192]{4,3,2,0,1:T(8,128)(2,1)} reshape(bf16[192,6144]{1,0:T(8,128)(2,1)} %convolution_convert_fusion) | data formatting | bytes 4718592 | tf_op jit(solution)/shard_map/convert_element_type | solution.py:85
  113.3 5.3 %copy.58 = bf16[16,1,12,32,192]{4,0,2,1,3:T(8,128)(2,1)} copy(bf16[16,1,12,32,192]{4,3,2,0,1:T(8,128)(2,1)} %convert_element_type.35) | data formatting | bytes 4718592 | tf_op jit(solution)/shard_map/convert_element_type | solution.py:85
  118.6 0.0 all-to-all-done
  118.6 0.0 copy-start.3
  118.6 7.6 %all-to-all-start.3 = ((bf16[32,16,1,12,192]{4,1,3,2,0:T(8,128)(2,1)}), bf16[32,16,1,12,192]{4,1,3,2,0:T(8,128)(2,1)}, u32[]{:S(2)}, u32[]{:S(2)}) async-start(bf16[32,16,1,12,192]{4,1,3,2,0:T(8,128)(2,1)} %bitcast.31), calls=%async_computation.3 | async-start | bytes 6291456 | tf_op jit(solution)/shard_map/all_to_all | solution.py:38
  126.2 0.5 broadcast.44
  126.7 0.7 reduce.2
  127.5 0.1 reshape.74
  127.6 0.0 copy-done.3
  127.6 40.4 %all-to-all-done.3 = bf16[32,16,1,12,192]{4,1,3,2,0:T(8,128)(2,1)} async-done(((bf16[32,16,1,12,192]{4,1,3,2,0:T(8,128)(2,1)}), bf16[32,16,1,12,192]{4,1,3,2,0:T(8,128)(2,1)}, u32[]{:S(2)}, u32[]{:S(2)}) %all-to-all-start.3) | async-done | bytes 2359328 | tf_op jit(solution)/shard_map/all_to_all | solution.py:38
  168.0 2.4 %reduce_sum.66 = bf16[16,12,192]{2,0,1:T(8,128)(2,1)S(1)} reduce(bf16[32,16,1,12,192]{4,1,3,2,0:T(8,128)(2,1)} %all-to-all-done.3, bf16[]{:T(256)} %constant.60.clone.1), dimensions={0,2}, to_apply=%region_6.7 | reduce | flops 1142784 | bytes 2433026 | tf_op jit(solution)/shard_map/reduce_sum | solution.py:39
  170.4 0.7 copy.56
  171.1 4.3 %all-to-all-start.4 = ((bf16[16,1,12,192]{3,2,1,0:T(8,128)(2,1)}), bf16[16,1,12,192]{3,2,1,0:T(8,128)(2,1)S(1)}, u32[]{:S(2)}, u32[]{:S(2)}) async-start(bf16[16,1,12,192]{3,2,1,0:T(8,128)(2,1)} %copy.56), calls=%async_computation.4 | async-start | bytes 262144 | tf_op jit(solution)/shard_map/all_to_all | solution.py:86
  175.4 0.1 select_reduce_fusion
  175.5 12.6 %all-to-all-done.4 = bf16[16,1,12,192]{3,2,1,0:T(8,128)(2,1)S(1)} async-done(((bf16[16,1,12,192]{3,2,1,0:T(8,128)(2,1)}), bf16[16,1,12,192]{3,2,1,0:T(8,128)(2,1)S(1)}, u32[]{:S(2)}, u32[]{:S(2)}) %all-to-all-start.4) | async-done | bytes 73760 | tf_op jit(solution)/shard_map/all_to_all | solution.py:86
  188.2 0.8 convolution_convert_fusion.2
  (10 shorter events, 0.2 us)
Async XLA Ops:
  0.0 101.8 %copy-start = (bf16[128,6144]{1,0:T(8,128)(2,1)S(1)}, bf16[128,6144]{1,0:T(8,128)(2,1)}, u32[]{:S(2)}) copy-start(bf16[128,6144]{1,0:T(8,128)(2,1)} %param.11) | copy-start | bytes 4718596
  34.5 7.6 %copy-start.2 = (bf16[24,192]{1,0:T(8,128)(2,1)S(1)}, bf16[24,192]{1,0:T(8,128)(2,1)}, u32[]{:S(2)}) copy-start(bf16[24,192]{1,0:T(8,128)(2,1)} %param.6) | copy-start | bytes 27652
  34.5 49.3 %all-to-all-start.2 = ((bf16[32,16,1,12,192]{4,1,3,2,0:T(8,128)(2,1)}), bf16[32,16,1,12,192]{4,1,3,2,0:T(8,128)(2,1)}, u32[]{:S(2)}, u32[]{:S(2)}) async-start(bf16[32,16,1,12,192]{4,1,3,2,0:T(8,128)(2,1)} %broadcast_in_dim.64), calls=%async_computation.2 | async-start | bytes 6291456 | tf_op jit(solution)/shard_map/all_to_all | solution.py:11
  83.9 34.7 %all-to-all-start = ((f32[32,1,192]{2,1,0:T(1,128)}), f32[32,1,192]{2,1,0:T(1,128)S(1)}, u32[]{:S(2)}, u32[]{:S(2)}) async-start(f32[32,1,192]{2,1,0:T(1,128)} %reshape.73), calls=%async_computation | async-start | bytes 65536 | tf_op jit(solution)/shard_map/all_to_all | solution.py:11
  93.0 6.3 %copy-start.1 = (bf16[6144,128]{1,0:T(8,128)(2,1)S(1)}, bf16[6144,128]{1,0:T(8,128)(2,1)}, u32[]{:S(2)}) copy-start(bf16[6144,128]{1,0:T(8,128)(2,1)} %param.9) | copy-start | bytes 4718596
  118.6 9.0 %copy-start.3 = (s32[24,2]{0,1:T(2,128)S(1)}, s32[24,2]{0,1:T(2,128)}, u32[]{:S(2)}) copy-start(s32[24,2]{0,1:T(2,128)} %param.7) | copy-start | bytes 580
  118.6 49.4 %all-to-all-start.3 = ((bf16[32,16,1,12,192]{4,1,3,2,0:T(8,128)(2,1)}), bf16[32,16,1,12,192]{4,1,3,2,0:T(8,128)(2,1)}, u32[]{:S(2)}, u32[]{:S(2)}) async-start(bf16[32,16,1,12,192]{4,1,3,2,0:T(8,128)(2,1)} %bitcast.31), calls=%async_computation.3 | async-start | bytes 6291456 | tf_op jit(solution)/shard_map/all_to_all | solution.py:38
  171.1 17.1 %all-to-all-start.4 = ((bf16[16,1,12,192]{3,2,1,0:T(8,128)(2,1)}), bf16[16,1,12,192]{3,2,1,0:T(8,128)(2,1)S(1)}, u32[]{:S(2)}, u32[]{:S(2)}) async-start(bf16[16,1,12,192]{3,2,1,0:T(8,128)(2,1)} %copy.56), calls=%async_computation.4 | async-start | bytes 262144 | tf_op jit(solution)/shard_map/all_to_all | solution.py:86
where the time goes:
time: 190 us; the launch traced here: 189 us
  waiting for transfers between devices  93.1 us (49%)
  blocking collectives  29.2 us (15%)
  local copies, waits for them, and re-layouts  28.8 us (15%)
  starting transfers between devices  23.3 us (12%)
  matrix products  10 us (5%)
  other arithmetic  4.44 us (2%)
    all_to_all x1, waiting for transfers between devices, sum_at_owner(): lax.all_to_all(blocks, axis, split_axis=0, concat_axis=0, tiled=True)  40.4 us
    all_to_all x2, waiting for transfers between devices, sent_to_all(): lax.all_to_all(jnp.broadcast_to(value[None], (peers, *value.shape)), axis...  40.1 us
    all_to_all x1, blocking collectives, local(): lax.all_to_all(spread.reshape(groups, per_group, capacity, -1), 'expert',...  29.2 us
    all_to_all x1, waiting for transfers between devices, local(): lax.all_to_all(shares.astype(jnp.bfloat16), 'expert', split_axis=0, conca...  12.6 us
    convert_element_type x2, local copies, waits for them, and re-layouts, local(): shares = sum_at_owner(term.astype(jnp.bfloat16), 'shard', 3)  11.8 us
    all_to_all x2, starting transfers between devices, sent_to_all(): lax.all_to_all(jnp.broadcast_to(value[None], (peers, *value.shape)), axis...  11.4 us
    all_to_all x1, starting transfers between devices, sum_at_owner(): lax.all_to_all(blocks, axis, split_axis=0, concat_axis=0, tiled=True)  7.63 us
    reshape x1, local copies, waits for them, and re-layouts, local(): lax.dynamic_index_in_dim(piece, local_k, 1, keepdims=False)  6.31 us
  transfers between devices with their start and end apart: 4, of which 3 were waited for; matrix products, arithmetic and copies ran while one was open for 18% of the time, Pallas kernels for 0%

commit v1 on v0

--- a/solution.py
+++ b/solution.py
@@ -4,6 +4,17 @@
 from jax.sharding import PartitionSpec as P
 
 FF_W = 8192
+
+
+def in_blocks(array, dim, size):
+    before, after = (array.shape[:dim], array.shape[dim + 1 :])
+    return jnp.moveaxis(array.reshape(*before, size, -1, *after), dim, 0)
+
+
+def in_order(blocks, dim):
+    blocks = jnp.moveaxis(blocks, 0, dim)
+    lengths = blocks.shape
+    return blocks.reshape(*lengths[:dim], lengths[dim] * lengths[dim + 1], *lengths[dim + 2 :])
 
 
 def sent_to_all(value, axis):
@@ -66,13 +77,15 @@
     logits = of_everyone(jnp.dot(tokens, router_piece, preferred_element_type=jnp.float32), "shard")
     bucket = jnp.dot(dispatch, tokens, preferred_element_type=jnp.float32).astype(jnp.bfloat16)
     spread = jnp.repeat(bucket.reshape(experts, capacity, -1), repeat, axis=0)
-    arrived = lax.all_to_all(
-        spread.reshape(groups, per_group, capacity, -1),
-        "expert",
-        split_axis=0,
-        concat_axis=0,
-        tiled=True,
-    )
+    x = spread.reshape(groups, per_group, capacity, -1)
+    devices, index = (lax.axis_size("expert"), lax.axis_index("expert"))
+    parts = in_blocks(x, 0, devices)
+    outs = [parts[index]]
+    for lap in range(1, devices):
+        sent = parts[index ^ lap]
+        outs.append(lax.ppermute(sent, "expert", [(i, i ^ lap) for i in range(devices)]))
+    parts = jnp.stack(outs)[index ^ jnp.arange(devices)]
+    arrived = in_order(parts, 0)
     piece = gather_directly(arrived, "shard", 3)
     count = piece.shape[3]
     chosen = lax.dynamic_index_in_dim(piece, local_k, 1, keepdims=False).reshape(rows_total, count)

time: 190 us -> 254 us (1.34)
  starting transfers between devices: 23.3 us -> 110 us
  blocking collectives: 29.2 us -> 0 us
  waiting for transfers between devices: 93.1 us -> 98.3 us
    ppermute x0 -> x15, starting transfers between devices: none -> 81.3 us  [local(): lax.ppermute(sent, 'expert', [(i, i ^ lap) for i in range(devices)])]
    all_to_all x1 -> x0, blocking collectives: 29.2 us -> none  [local(): lax.all_to_all(spread.reshape(groups, per_group, capacity, -1), 'expert',...]
    all_to_all x1, starting transfers between devices: 4.33 us -> 9.78 us  [local(): lax.all_to_all(shares.astype(jnp.bfloat16), 'expert', split_axis=0, conca...]
    ppermute x0 -> x15, waiting for transfers between devices: none -> 5.21 us  [local(): lax.ppermute(sent, 'expert', [(i, i ^ lap) for i in range(devices)])]
  transfers between devices with their start and end apart: 4 -> 19, of which waited for: 3 -> 4; matrix products, arithmetic and copies ran while one was open for 18% -> 13% of each run, Pallas kernels for 0% -> 0%
where the time goes in v1:
time: 254 us; the launch traced here: 253 us
  starting transfers between devices  110 us (43%)
  waiting for transfers between devices  98.3 us (39%)
  local copies, waits for them, and re-layouts  29.4 us (12%)
  matrix products  10 us (4%)
  other arithmetic  4.45 us (2%)
    ppermute x15, starting transfers between devices, local(): lax.ppermute(sent, 'expert', [(i, i ^ lap) for i in range(devices)])  81.3 us
    all_to_all x1, waiting for transfers between devices, sum_at_owner(): lax.all_to_all(blocks, axis, split_axis=0, concat_axis=0, tiled=True)  40.4 us
    all_to_all x2, waiting for transfers between devices, sent_to_all(): lax.all_to_all(jnp.broadcast_to(value[None], (peers, *value.shape)), axis...  40.1 us
    all_to_all x1, waiting for transfers between devices, local(): lax.all_to_all(shares.astype(jnp.bfloat16), 'expert', split_axis=0, conca...  12.6 us
    convert_element_type x2, local copies, waits for them, and re-layouts, local(): shares = sum_at_owner(term.astype(jnp.bfloat16), 'shard', 3)  11.7 us
    all_to_all x2, starting transfers between devices, sent_to_all(): lax.all_to_all(jnp.broadcast_to(value[None], (peers, *value.shape)), axis...  11.4 us
    all_to_all x1, starting transfers between devices, local(): lax.all_to_all(shares.astype(jnp.bfloat16), 'expert', split_axis=0, conca...  9.78 us
    all_to_all x1, starting transfers between devices, sum_at_owner(): lax.all_to_all(blocks, axis, split_axis=0, concat_axis=0, tiled=True)  7.63 us
  transfers between devices with their start and end apart: 19, of which 4 were waited for; matrix products, arithmetic and copies ran while one was open for 13% of the time, Pallas kernels for 0%

profile of v1, /device:TPU:32, one launch (start us, length us, event | category | flops | bytes accessed | tf_op | source)
XLA Modules:
  0.0 252.9 jit_solution(14032363248070942966)
XLA Ops:
  0.0 0.9 copy.59
  0.9 0.1 eq.23
  1.1 0.2 select_reduce_fusion.1
  1.3 0.1 reduce_sum.62
  1.5 0.7 multiply_add_fusion
  2.2 0.1 fusion.7
  2.3 0.9 convolution_convert_fusion.1
  3.3 0.1 dynamic-slice_bitcast_fusion
  3.4 7.4 %collective-permute-start = (bf16[1,1,12,192]{3,2,1,0:T(8,128)(2,1)S(1)}, bf16[1,1,12,192]{3,2,1,0:T(8,128)(2,1)S(1)}, u32[]{:S(2)}, u32[]{:S(2)}) collective-permute-start(bf16[1,1,12,192]{3,2,1,0:T(8,128)(2,1)S(1)} %get-tuple-element.19), channel_id=1, source_target_pairs={{0,32},{32,0},{64,96},{96,64},{128,160},{160,128},{192,224},{224,1... | collective-permute-start | bytes 13832 | tf_op jit(solution)/shard_map/ppermute | solution.py:86
  10.8 1.9 collective-permute-start.1
  12.7 3.4 %collective-permute-start.2 = (bf16[1,1,12,192]{3,2,1,0:T(8,128)(2,1)S(1)}, bf16[1,1,12,192]{3,2,1,0:T(8,128)(2,1)S(1)}, u32[]{:S(2)}, u32[]{:S(2)}) collective-permute-start(bf16[1,1,12,192]{3,2,1,0:T(8,128)(2,1)S(1)} %get-tuple-element.17), channel_id=1, source_target_pairs={{0,96},{32,64},{64,32},{96,0},{128,224},{160,192},{192,160},{224,1... | collective-permute-start | bytes 13832 | tf_op jit(solution)/shard_map/ppermute | solution.py:86
  16.1 6.0 %collective-permute-start.3 = (bf16[1,1,12,192]{3,2,1,0:T(8,128)(2,1)S(1)}, bf16[1,1,12,192]{3,2,1,0:T(8,128)(2,1)S(1)}, u32[]{:S(2)}, u32[]{:S(2)}) collective-permute-start(bf16[1,1,12,192]{3,2,1,0:T(8,128)(2,1)S(1)} %get-tuple-element.16), channel_id=1, source_target_pairs={{0,128},{32,160},{64,192},{96,224},{128,0},{160,32},{192,64},{224,... | collective-permute-start | bytes 13832 | tf_op jit(solution)/shard_map/ppermute | solution.py:86
  22.1 5.2 %collective-permute-start.4 = (bf16[1,1,12,192]{3,2,1,0:T(8,128)(2,1)S(1)}, bf16[1,1,12,192]{3,2,1,0:T(8,128)(2,1)S(1)}, u32[]{:S(2)}, u32[]{:S(2)}) collective-permute-start(bf16[1,1,12,192]{3,2,1,0:T(8,128)(2,1)S(1)} %get-tuple-element.15), channel_id=1, source_target_pairs={{0,160},{32,128},{64,224},{96,192},{128,32},{160,0},{192,96},{224,... | collective-permute-start | bytes 13832 | tf_op jit(solution)/shard_map/ppermute | solution.py:86
  27.4 6.4 %collective-permute-start.5 = (bf16[1,1,12,192]{3,2,1,0:T(8,128)(2,1)S(1)}, bf16[1,1,12,192]{3,2,1,0:T(8,128)(2,1)S(1)}, u32[]{:S(2)}, u32[]{:S(2)}) collective-permute-start(bf16[1,1,12,192]{3,2,1,0:T(8,128)(2,1)S(1)} %get-tuple-element.14), channel_id=1, source_target_pairs={{0,192},{32,224},{64,128},{96,160},{128,64},{160,96},{192,0},{224,... | collective-permute-start | bytes 13832 | tf_op jit(solution)/shard_map/ppermute | solution.py:86
  33.8 3.7 %collective-permute-start.6 = (bf16[1,1,12,192]{3,2,1,0:T(8,128)(2,1)S(1)}, bf16[1,1,12,192]{3,2,1,0:T(8,128)(2,1)S(1)}, u32[]{:S(2)}, u32[]{:S(2)}) collective-permute-start(bf16[1,1,12,192]{3,2,1,0:T(8,128)(2,1)S(1)} %get-tuple-element.13), channel_id=1, source_target_pairs={{0,224},{32,192},{64,160},{96,128},{128,96},{160,64},{192,32},{224... | collective-permute-start | bytes 13832 | tf_op jit(solution)/shard_map/ppermute | solution.py:86
  37.5 11.4 %collective-permute-start.7 = (bf16[1,1,12,192]{3,2,1,0:T(8,128)(2,1)S(1)}, bf16[1,1,12,192]{3,2,1,0:T(8,128)(2,1)S(1)}, u32[]{:S(2)}, u32[]{:S(2)}) collective-permute-start(bf16[1,1,12,192]{3,2,1,0:T(8,128)(2,1)S(1)} %get-tuple-element.12), channel_id=1, source_target_pairs={{0,256},{32,288},{64,320},{96,352},{128,384},{160,416},{192,448},{... | collective-permute-start | bytes 13832 | tf_op jit(solution)/shard_map/ppermute | solution.py:86
  48.9 4.7 %collective-permute-start.8 = (bf16[1,1,12,192]{3,2,1,0:T(8,128)(2,1)S(1)}, bf16[1,1,12,192]{3,2,1,0:T(8,128)(2,1)S(1)}, u32[]{:S(2)}, u32[]{:S(2)}) collective-permute-start(bf16[1,1,12,192]{3,2,1,0:T(8,128)(2,1)S(1)} %get-tuple-element.11), channel_id=1, source_target_pairs={{0,288},{32,256},{64,352},{96,320},{128,416},{160,384},{192,480},{... | collective-permute-start | bytes 13832 | tf_op jit(solution)/shard_map/ppermute | solution.py:86
  53.6 5.0 %collective-permute-start.9 = (bf16[1,1,12,192]{3,2,1,0:T(8,128)(2,1)S(1)}, bf16[1,1,12,192]{3,2,1,0:T(8,128)(2,1)S(1)}, u32[]{:S(2)}, u32[]{:S(2)}) collective-permute-start(bf16[1,1,12,192]{3,2,1,0:T(8,128)(2,1)S(1)} %get-tuple-element.10), channel_id=1, source_target_pairs={{0,320},{32,352},{64,256},{96,288},{128,448},{160,480},{192,384},{... | collective-permute-start | bytes 13832 | tf_op jit(solution)/shard_map/ppermute | solution.py:86
  58.6 6.4 %collective-permute-start.10 = (bf16[1,1,12,192]{3,2,1,0:T(8,128)(2,1)S(1)}, bf16[1,1,12,192]{3,2,1,0:T(8,128)(2,1)S(1)}, u32[]{:S(2)}, u32[]{:S(2)}) collective-permute-start(bf16[1,1,12,192]{3,2,1,0:T(8,128)(2,1)S(1)} %get-tuple-element.9), channel_id=1, source_target_pairs={{0,352},{32,320},{64,288},{96,256},{128,480},{160,448},{192,416},{... | collective-permute-start | bytes 13832 | tf_op jit(solution)/shard_map/ppermute | solution.py:86
  65.0 5.0 %collective-permute-start.11 = (bf16[1,1,12,192]{3,2,1,0:T(8,128)(2,1)S(1)}, bf16[1,1,12,192]{3,2,1,0:T(8,128)(2,1)S(1)}, u32[]{:S(2)}, u32[]{:S(2)}) collective-permute-start(bf16[1,1,12,192]{3,2,1,0:T(8,128)(2,1)S(1)} %get-tuple-element.8), channel_id=1, source_target_pairs={{0,384},{32,416},{64,448},{96,480},{128,256},{160,288},{192,320},{... | collective-permute-start | bytes 13832 | tf_op jit(solution)/shard_map/ppermute | solution.py:86
  70.1 6.1 %collective-permute-start.12 = (bf16[1,1,12,192]{3,2,1,0:T(8,128)(2,1)S(1)}, bf16[1,1,12,192]{3,2,1,0:T(8,128)(2,1)S(1)}, u32[]{:S(2)}, u32[]{:S(2)}) collective-permute-start(bf16[1,1,12,192]{3,2,1,0:T(8,128)(2,1)S(1)} %get-tuple-element.7), channel_id=1, source_target_pairs={{0,416},{32,384},{64,480},{96,448},{128,288},{160,256},{192,352},{... | collective-permute-start | bytes 13832 | tf_op jit(solution)/shard_map/ppermute | solution.py:86
  76.2 5.6 %collective-permute-start.13 = (bf16[1,1,12,192]{3,2,1,0:T(8,128)(2,1)S(1)}, bf16[1,1,12,192]{3,2,1,0:T(8,128)(2,1)S(1)}, u32[]{:S(2)}, u32[]{:S(2)}) collective-permute-start(bf16[1,1,12,192]{3,2,1,0:T(8,128)(2,1)S(1)} %get-tuple-element.6), channel_id=1, source_target_pairs={{0,448},{32,480},{64,384},{96,416},{128,320},{160,352},{192,256},{... | collective-permute-start | bytes 13832 | tf_op jit(solution)/shard_map/ppermute | solution.py:86
  81.8 3.3 %collective-permute-start.14 = (bf16[1,1,12,192]{3,2,1,0:T(8,128)(2,1)S(1)}, bf16[1,1,12,192]{3,2,1,0:T(8,128)(2,1)S(1)}, u32[]{:S(2)}, u32[]{:S(2)}) collective-permute-start(bf16[1,1,12,192]{3,2,1,0:T(8,128)(2,1)S(1)} %get-tuple-element.5), channel_id=1, source_target_pairs={{0,480},{32,448},{64,416},{96,384},{128,352},{160,320},{192,288},{... | collective-permute-start | bytes 13832 | tf_op jit(solution)/shard_map/ppermute | solution.py:86
  85.2 5.2 %collective-permute-done.14 = bf16[1,1,12,192]{3,2,1,0:T(8,128)(2,1)S(1)} collective-permute-done((bf16[1,1,12,192]{3,2,1,0:T(8,128)(2,1)S(1)}, bf16[1,1,12,192]{3,2,1,0:T(8,128)(2,1)S(1)}, u32[]{:S(2)}, u32[]{:S(2)}) %collective-permute-start.14) | collective-permute-done | bytes 4640 | tf_op jit(solution)/shard_map/ppermute | solution.py:86
  90.4 0.6 gather_fusion
  91.0 2.0 broadcast_in_dim.64
  93.0 7.6 %all-to-all-start.1 = ((bf16[32,16,1,12,192]{4,1,3,2,0:T(8,128)(2,1)}), bf16[32,16,1,12,192]{4,1,3,2,0:T(8,128)(2,1)}, u32[]{:S(2)}, u32[]{:S(2)}) async-start(bf16[32,16,1,12,192]{4,1,3,2,0:T(8,128)(2,1)} %broadcast_in_dim.64), calls=%async_computation.1 | async-start | bytes 6291456 | tf_op jit(solution)/shard_map/all_to_all | solution.py:22
  100.6 0.9 convolution_bitcast_fusion
  101.5 0.8 reshape.104
  102.3 40.1 %all-to-all-done.1 = bf16[32,16,1,12,192]{4,1,3,2,0:T(8,128)(2,1)} async-done(((bf16[32,16,1,12,192]{4,1,3,2,0:T(8,128)(2,1)}), bf16[32,16,1,12,192]{4,1,3,2,0:T(8,128)(2,1)}, u32[]{:S(2)}, u32[]{:S(2)}) %all-to-all-start.1) | async-done | bytes 2359328 | tf_op jit(solution)/shard_map/all_to_all | solution.py:22
  142.4 3.8 %all-to-all-start = ((f32[32,1,192]{2,1,0:T(1,128)}), f32[32,1,192]{2,1,0:T(1,128)S(1)}, u32[]{:S(2)}, u32[]{:S(2)}) async-start(f32[32,1,192]{2,1,0:T(1,128)} %reshape.104), calls=%async_computation | async-start | bytes 65536 | tf_op jit(solution)/shard_map/all_to_all | solution.py:22
  146.2 5.3 %copy.62 = bf16[16,1,12,32,192]{4,3,2,0,1:T(8,128)(2,1)} copy(bf16[16,1,12,32,192]{4,0,2,1,3:T(8,128)(2,1)} %bitcast.34) | data formatting | bytes 4718592 | tf_op jit(solution)/shard_map/transpose | solution.py:33
  151.5 6.3 %reshape.83 = bf16[192,6144]{1,0:T(8,128)(2,1)} reshape(bf16[16,1,12,32,192]{4,3,2,0,1:T(8,128)(2,1)} %copy.62) | data formatting | bytes 4718592 | tf_op jit(solution)/shard_map/reshape | solution.py:91
  157.8 2.4 fusion.11
  160.3 5.0 %convolution_convert_fusion = bf16[192,6144]{1,0:T(8,128)(2,1)} fusion(bf16[128,6144]{1,0:T(8,128)(2,1)S(1)} %copy-done, bf16[192,6144]{1,0:T(8,128)(2,1)} %reshape.83, bf16[6144,128]{1,0:T(8,128)(2,1)} %param.10, f32[192,128]{1,0:T(8,128)S(1)} %fusion.11), kind=kOutput, calls=%fused_computation.1 | convolution fusion | flops 605306880 | bytes 7962624 | tf_op jit(solution)/shard_map/dot_general | solution.py:95
  165.3 6.4 %convert_element_type.35 = bf16[16,1,12,32,192]{4,3,2,0,1:T(8,128)(2,1)} reshape(bf16[192,6144]{1,0:T(8,128)(2,1)} %convolution_convert_fusion) | data formatting | bytes 4718592 | tf_op jit(solution)/shard_map/convert_element_type | solution.py:98
  171.7 5.3 %copy.66 = bf16[16,1,12,32,192]{4,0,2,1,3:T(8,128)(2,1)} copy(bf16[16,1,12,32,192]{4,3,2,0,1:T(8,128)(2,1)} %convert_element_type.35) | data formatting | bytes 4718592 | tf_op jit(solution)/shard_map/convert_element_type | solution.py:98
  177.0 7.6 %all-to-all-start.2 = ((bf16[32,16,1,12,192]{4,1,3,2,0:T(8,128)(2,1)}), bf16[32,16,1,12,192]{4,1,3,2,0:T(8,128)(2,1)}, u32[]{:S(2)}, u32[]{:S(2)}) async-start(bf16[32,16,1,12,192]{4,1,3,2,0:T(8,128)(2,1)} %bitcast.93), calls=%async_computation.2 | async-start | bytes 6291456 | tf_op jit(solution)/shard_map/all_to_all | solution.py:49
  184.7 0.5 broadcast.80
  185.2 0.7 reduce.2
  185.9 0.1 reshape.105
  186.1 40.4 %all-to-all-done.2 = bf16[32,16,1,12,192]{4,1,3,2,0:T(8,128)(2,1)} async-done(((bf16[32,16,1,12,192]{4,1,3,2,0:T(8,128)(2,1)}), bf16[32,16,1,12,192]{4,1,3,2,0:T(8,128)(2,1)}, u32[]{:S(2)}, u32[]{:S(2)}) %all-to-all-start.2) | async-done | bytes 2359328 | tf_op jit(solution)/shard_map/all_to_all | solution.py:49
  226.4 2.4 reduce_sum.66
  228.9 0.7 copy.64
  229.6 9.8 %all-to-all-start.3 = ((bf16[16,1,12,192]{3,2,1,0:T(8,128)(2,1)}), bf16[16,1,12,192]{3,2,1,0:T(8,128)(2,1)S(1)}, u32[]{:S(2)}, u32[]{:S(2)}) async-start(bf16[16,1,12,192]{3,2,1,0:T(8,128)(2,1)} %copy.64), calls=%async_computation.3 | async-start | bytes 262144 | tf_op jit(solution)/shard_map/all_to_all | solution.py:99
  239.4 0.1 select_reduce_fusion
  239.5 12.6 %all-to-all-done.3 = bf16[16,1,12,192]{3,2,1,0:T(8,128)(2,1)S(1)} async-done(((bf16[16,1,12,192]{3,2,1,0:T(8,128)(2,1)}), bf16[16,1,12,192]{3,2,1,0:T(8,128)(2,1)S(1)}, u32[]{:S(2)}, u32[]{:S(2)}) %all-to-all-start.3) | async-done | bytes 73760 | tf_op jit(solution)/shard_map/all_to_all | solution.py:99
  252.1 0.8 convolution_convert_fusion.2
  (53 shorter events, 0.5 us)
Async XLA Ops:
  0.0 160.2 %copy-start = (bf16[128,6144]{1,0:T(8,128)(2,1)S(1)}, bf16[128,6144]{1,0:T(8,128)(2,1)}, u32[]{:S(2)}) copy-start(bf16[128,6144]{1,0:T(8,128)(2,1)} %param.11) | copy-start | bytes 4718596
  3.4 24.0 %collective-permute-start = (bf16[1,1,12,192]{3,2,1,0:T(8,128)(2,1)S(1)}, bf16[1,1,12,192]{3,2,1,0:T(8,128)(2,1)S(1)}, u32[]{:S(2)}, u32[]{:S(2)}) collective-permute-start(bf16[1,1,12,192]{3,2,1,0:T(8,128)(2,1)S(1)} %get-tuple-element.19), channel_id=1, source_target_pairs={{0,32},{32,0},{64,96},{96,64},{128,160},{160,128},{192,224},{224,1... | collective-permute-start | bytes 13832 | tf_op jit(solution)/shard_map/ppermute | solution.py:86
  10.8 23.0 %collective-permute-start.1 = (bf16[1,1,12,192]{3,2,1,0:T(8,128)(2,1)S(1)}, bf16[1,1,12,192]{3,2,1,0:T(8,128)(2,1)S(1)}, u32[]{:S(2)}, u32[]{:S(2)}) collective-permute-start(bf16[1,1,12,192]{3,2,1,0:T(8,128)(2,1)S(1)} %get-tuple-element.18), channel_id=1, source_target_pairs={{0,64},{32,96},{64,0},{96,32},{128,192},{160,224},{192,128},{224,1... | collective-permute-start | bytes 13832 | tf_op jit(solution)/shard_map/ppermute | solution.py:86
  12.7 24.8 %collective-permute-start.2 = (bf16[1,1,12,192]{3,2,1,0:T(8,128)(2,1)S(1)}, bf16[1,1,12,192]{3,2,1,0:T(8,128)(2,1)S(1)}, u32[]{:S(2)}, u32[]{:S(2)}) collective-permute-start(bf16[1,1,12,192]{3,2,1,0:T(8,128)(2,1)S(1)} %get-tuple-element.17), channel_id=1, source_target_pairs={{0,96},{32,64},{64,32},{96,0},{128,224},{160,192},{192,160},{224,1... | collective-permute-start | bytes 13832 | tf_op jit(solution)/shard_map/ppermute | solution.py:86
  16.1 32.8 %collective-permute-start.3 = (bf16[1,1,12,192]{3,2,1,0:T(8,128)(2,1)S(1)}, bf16[1,1,12,192]{3,2,1,0:T(8,128)(2,1)S(1)}, u32[]{:S(2)}, u32[]{:S(2)}) collective-permute-start(bf16[1,1,12,192]{3,2,1,0:T(8,128)(2,1)S(1)} %get-tuple-element.16), channel_id=1, source_target_pairs={{0,128},{32,160},{64,192},{96,224},{128,0},{160,32},{192,64},{224,... | collective-permute-start | bytes 13832 | tf_op jit(solution)/shard_map/ppermute | solution.py:86
  22.1 31.5 %collective-permute-start.4 = (bf16[1,1,12,192]{3,2,1,0:T(8,128)(2,1)S(1)}, bf16[1,1,12,192]{3,2,1,0:T(8,128)(2,1)S(1)}, u32[]{:S(2)}, u32[]{:S(2)}) collective-permute-start(bf16[1,1,12,192]{3,2,1,0:T(8,128)(2,1)S(1)} %get-tuple-element.15), channel_id=1, source_target_pairs={{0,160},{32,128},{64,224},{96,192},{128,32},{160,0},{192,96},{224,... | collective-permute-start | bytes 13832 | tf_op jit(solution)/shard_map/ppermute | solution.py:86
  27.4 31.2 %collective-permute-start.5 = (bf16[1,1,12,192]{3,2,1,0:T(8,128)(2,1)S(1)}, bf16[1,1,12,192]{3,2,1,0:T(8,128)(2,1)S(1)}, u32[]{:S(2)}, u32[]{:S(2)}) collective-permute-start(bf16[1,1,12,192]{3,2,1,0:T(8,128)(2,1)S(1)} %get-tuple-element.14), channel_id=1, source_target_pairs={{0,192},{32,224},{64,128},{96,160},{128,64},{160,96},{192,0},{224,... | collective-permute-start | bytes 13832 | tf_op jit(solution)/shard_map/ppermute | solution.py:86
  33.8 31.2 %collective-permute-start.6 = (bf16[1,1,12,192]{3,2,1,0:T(8,128)(2,1)S(1)}, bf16[1,1,12,192]{3,2,1,0:T(8,128)(2,1)S(1)}, u32[]{:S(2)}, u32[]{:S(2)}) collective-permute-start(bf16[1,1,12,192]{3,2,1,0:T(8,128)(2,1)S(1)} %get-tuple-element.13), channel_id=1, source_target_pairs={{0,224},{32,192},{64,160},{96,128},{128,96},{160,64},{192,32},{224... | collective-permute-start | bytes 13832 | tf_op jit(solution)/shard_map/ppermute | solution.py:86
  37.5 32.6 %collective-permute-start.7 = (bf16[1,1,12,192]{3,2,1,0:T(8,128)(2,1)S(1)}, bf16[1,1,12,192]{3,2,1,0:T(8,128)(2,1)S(1)}, u32[]{:S(2)}, u32[]{:S(2)}) collective-permute-start(bf16[1,1,12,192]{3,2,1,0:T(8,128)(2,1)S(1)} %get-tuple-element.12), channel_id=1, source_target_pairs={{0,256},{32,288},{64,320},{96,352},{128,384},{160,416},{192,448},{... | collective-permute-start | bytes 13832 | tf_op jit(solution)/shard_map/ppermute | solution.py:86
  48.9 27.3 %collective-permute-start.8 = (bf16[1,1,12,192]{3,2,1,0:T(8,128)(2,1)S(1)}, bf16[1,1,12,192]{3,2,1,0:T(8,128)(2,1)S(1)}, u32[]{:S(2)}, u32[]{:S(2)}) collective-permute-start(bf16[1,1,12,192]{3,2,1,0:T(8,128)(2,1)S(1)} %get-tuple-element.11), channel_id=1, source_target_pairs={{0,288},{32,256},{64,352},{96,320},{128,416},{160,384},{192,480},{... | collective-permute-start | bytes 13832 | tf_op jit(solution)/shard_map/ppermute | solution.py:86
  53.6 28.2 %collective-permute-start.9 = (bf16[1,1,12,192]{3,2,1,0:T(8,128)(2,1)S(1)}, bf16[1,1,12,192]{3,2,1,0:T(8,128)(2,1)S(1)}, u32[]{:S(2)}, u32[]{:S(2)}) collective-permute-start(bf16[1,1,12,192]{3,2,1,0:T(8,128)(2,1)S(1)} %get-tuple-element.10), channel_id=1, source_target_pairs={{0,320},{32,352},{64,256},{96,288},{128,448},{160,480},{192,384},{... | collective-permute-start | bytes 13832 | tf_op jit(solution)/shard_map/ppermute | solution.py:86
  58.6 26.5 %collective-permute-start.10 = (bf16[1,1,12,192]{3,2,1,0:T(8,128)(2,1)S(1)}, bf16[1,1,12,192]{3,2,1,0:T(8,128)(2,1)S(1)}, u32[]{:S(2)}, u32[]{:S(2)}) collective-permute-start(bf16[1,1,12,192]{3,2,1,0:T(8,128)(2,1)S(1)} %get-tuple-element.9), channel_id=1, source_target_pairs={{0,352},{32,320},{64,288},{96,256},{128,480},{160,448},{192,416},{... | collective-permute-start | bytes 13832 | tf_op jit(solution)/shard_map/ppermute | solution.py:86
  65.0 20.1 %collective-permute-start.11 = (bf16[1,1,12,192]{3,2,1,0:T(8,128)(2,1)S(1)}, bf16[1,1,12,192]{3,2,1,0:T(8,128)(2,1)S(1)}, u32[]{:S(2)}, u32[]{:S(2)}) collective-permute-start(bf16[1,1,12,192]{3,2,1,0:T(8,128)(2,1)S(1)} %get-tuple-element.8), channel_id=1, source_target_pairs={{0,384},{32,416},{64,448},{96,480},{128,256},{160,288},{192,320},{... | collective-permute-start | bytes 13832 | tf_op jit(solution)/shard_map/ppermute | solution.py:86
  70.1 15.1 %collective-permute-start.12 = (bf16[1,1,12,192]{3,2,1,0:T(8,128)(2,1)S(1)}, bf16[1,1,12,192]{3,2,1,0:T(8,128)(2,1)S(1)}, u32[]{:S(2)}, u32[]{:S(2)}) collective-permute-start(bf16[1,1,12,192]{3,2,1,0:T(8,128)(2,1)S(1)} %get-tuple-element.7), channel_id=1, source_target_pairs={{0,416},{32,384},{64,480},{96,448},{128,288},{160,256},{192,352},{... | collective-permute-start | bytes 13832 | tf_op jit(solution)/shard_map/ppermute | solution.py:86
  76.2 9.0 %collective-permute-start.13 = (bf16[1,1,12,192]{3,2,1,0:T(8,128)(2,1)S(1)}, bf16[1,1,12,192]{3,2,1,0:T(8,128)(2,1)S(1)}, u32[]{:S(2)}, u32[]{:S(2)}) collective-permute-start(bf16[1,1,12,192]{3,2,1,0:T(8,128)(2,1)S(1)} %get-tuple-element.6), channel_id=1, source_target_pairs={{0,448},{32,480},{64,384},{96,416},{128,320},{160,352},{192,256},{... | collective-permute-start | bytes 13832 | tf_op jit(solution)/shard_map/ppermute | solution.py:86
  81.8 8.6 %collective-permute-start.14 = (bf16[1,1,12,192]{3,2,1,0:T(8,128)(2,1)S(1)}, bf16[1,1,12,192]{3,2,1,0:T(8,128)(2,1)S(1)}, u32[]{:S(2)}, u32[]{:S(2)}) collective-permute-start(bf16[1,1,12,192]{3,2,1,0:T(8,128)(2,1)S(1)} %get-tuple-element.5), channel_id=1, source_target_pairs={{0,480},{32,448},{64,416},{96,384},{128,352},{160,320},{192,288},{... | collective-permute-start | bytes 13832 | tf_op jit(solution)/shard_map/ppermute | solution.py:86
  93.0 7.6 %copy-start.2 = (bf16[24,192]{1,0:T(8,128)(2,1)S(1)}, bf16[24,192]{1,0:T(8,128)(2,1)}, u32[]{:S(2)}) copy-start(bf16[24,192]{1,0:T(8,128)(2,1)} %param.6) | copy-start | bytes 27652
  93.0 49.3 %all-to-all-start.1 = ((bf16[32,16,1,12,192]{4,1,3,2,0:T(8,128)(2,1)}), bf16[32,16,1,12,192]{4,1,3,2,0:T(8,128)(2,1)}, u32[]{:S(2)}, u32[]{:S(2)}) async-start(bf16[32,16,1,12,192]{4,1,3,2,0:T(8,128)(2,1)} %broadcast_in_dim.64), calls=%async_computation.1 | async-start | bytes 6291456 | tf_op jit(solution)/shard_map/all_to_all | solution.py:22
  142.4 34.7 %all-to-all-start = ((f32[32,1,192]{2,1,0:T(1,128)}), f32[32,1,192]{2,1,0:T(1,128)S(1)}, u32[]{:S(2)}, u32[]{:S(2)}) async-start(f32[32,1,192]{2,1,0:T(1,128)} %reshape.104), calls=%async_computation | async-start | bytes 65536 | tf_op jit(solution)/shard_map/all_to_all | solution.py:22
  151.5 6.3 %copy-start.1 = (bf16[6144,128]{1,0:T(8,128)(2,1)S(1)}, bf16[6144,128]{1,0:T(8,128)(2,1)}, u32[]{:S(2)}) copy-start(bf16[6144,128]{1,0:T(8,128)(2,1)} %param.9) | copy-start | bytes 4718596
  177.0 9.0 %copy-start.3 = (s32[24,2]{0,1:T(2,128)S(1)}, s32[24,2]{0,1:T(2,128)}, u32[]{:S(2)}) copy-start(s32[24,2]{0,1:T(2,128)} %param.7) | copy-start | bytes 580
  177.0 49.4 %all-to-all-start.2 = ((bf16[32,16,1,12,192]{4,1,3,2,0:T(8,128)(2,1)}), bf16[32,16,1,12,192]{4,1,3,2,0:T(8,128)(2,1)}, u32[]{:S(2)}, u32[]{:S(2)}) async-start(bf16[32,16,1,12,192]{4,1,3,2,0:T(8,128)(2,1)} %bitcast.93), calls=%async_computation.2 | async-start | bytes 6291456 | tf_op jit(solution)/shard_map/all_to_all | solution.py:49
  229.6 22.5 %all-to-all-start.3 = ((bf16[16,1,12,192]{3,2,1,0:T(8,128)(2,1)}), bf16[16,1,12,192]{3,2,1,0:T(8,128)(2,1)S(1)}, u32[]{:S(2)}, u32[]{:S(2)}) async-start(bf16[16,1,12,192]{3,2,1,0:T(8,128)(2,1)} %copy.64), calls=%async_computation.3 | async-start | bytes 262144 | tf_op jit(solution)/shard_map/all_to_all | solution.py:99
